TPU v7x, 32 devices: a whole 2x2x4 slice. The times are simulated.
32 devices in a mesh: seq: 4 (over y, core), batch: 8 (over z, x).
Axes of the slice: x: 2, y: 2, z: 4, core: 2. Of those that a mesh axis runs over, the one named last changes fastest.
Arguments:
- waveforms: bfloat16 [8, 24, 16000], P('batch', 'seq'), may hold values from -6 to 6
- clip_lengths: int32 [8, 4], P('batch'), may hold values from 1 to 6, as said below
- block_starts: int32 [8, 24], P('batch'), may hold values from 0 to 744, as said below
- conv_first: bfloat16 [384, 1280], P('batch'), may hold values from -0.3125 to 0.3125
- bias_first: float32 [1280], replicated, may hold values from -3 to 3
- conv_second: bfloat16 [3840, 1280], replicated, may hold values from -0.09375 to 0.09375
- bias_second: float32 [1280], replicated, may hold values from -3 to 3
- norm_gain: float32 [1280], replicated, may hold values from 0.25 to 1.75
- projector: bfloat16 [1280, 4096], P(None, 'seq'), may hold values from -0.15625 to 0.15625
- proj_bias: float32 [4096], P('seq'), may hold values from -3 to 3
Outputs:
- audio_rows: bfloat16 [8, 768, 4096], P('batch', 'seq')
Inputs may be any that keep to these rules, and one draw needn't show every extreme that they name: `clip_lengths`: the lengths of a sequence's 4 clips sum to 12, and one clip has 6 blocks. `block_starts`: A clip's live blocks start 24 positions apart, in slot order; live blocks of a sequence occupy disjoint positions; entries of dead slots are 0.
All inputs are finite; a program needn't handle non-finite values.
Results may differ from a plain program's by a relative error of at most 0.0055.
Values may be sent and summed in bfloat16 or wider, within the bound.
A program may use at most 64 MiB of HBM per device.

v0:
```python
import jax
import jax.numpy as jnp
import numpy as np
from jax import lax
from jax.sharding import PartitionSpec as P

MEL = 128
WIDTH = 1280
HOP = 160
WINDOW = 400
BINS = 201
FRAMES = 96
TOK = 24
OWN_ROWS = 192


def hertz_to_mel(hertz):
    return np.where(
        hertz < 1000.0,
        hertz / (200.0 / 3.0),
        15.0 + np.log(np.maximum(hertz, 1.0) / 1000.0) / (np.log(6.4) / 27.0),
    )


def mel_to_hertz(mels):
    return np.where(
        mels < 15.0, mels * 200.0 / 3.0, 1000.0 * np.exp((mels - 15.0) * np.log(6.4) / 27.0)
    )


def spectral_tables():
    sample_rate = HOP * 100.0
    sample_index = np.arange(WINDOW)
    hann = 0.5 - 0.5 * np.cos(2.0 * np.pi * sample_index / WINDOW)
    angles = 2.0 * np.pi * np.outer(sample_index, np.arange(BINS)) / WINDOW
    dft_basis = np.concatenate(
        [hann[:, None] * np.cos(angles), -hann[:, None] * np.sin(angles)], axis=1
    )
    edges = mel_to_hertz(
        np.linspace(0.0, float(hertz_to_mel(np.array(sample_rate / 2.0))), MEL + 2)
    )
    bin_hertz = np.arange(BINS) * sample_rate / WINDOW
    rising = (bin_hertz[:, None] - edges[None, :-2]) / (edges[1:-1] - edges[:-2])[None, :]
    falling = (edges[None, 2:] - bin_hertz[:, None]) / (edges[2:] - edges[1:-1])[None, :]
    filters = (
        np.maximum(0.0, np.minimum(rising, falling)) * (2.0 / (edges[2:] - edges[:-2]))[None, :]
    )
    return (jnp.asarray(dft_basis.astype(np.float32)), jnp.asarray(filters.astype(np.float32)))


def encode(blocks_in, tables, conv_first, bias_first, conv_second, bias_second, norm_gain):
    dft_basis, filters = tables
    block_count = blocks_in.shape[0]
    segments = blocks_in.astype(jnp.float32).reshape(block_count, FRAMES + 4, HOP)
    frames = jnp.concatenate(
        [
            segments[:, :FRAMES],
            segments[:, 1 : FRAMES + 1],
            segments[:, 2 : FRAMES + 2, : HOP // 2],
        ],
        axis=2,
    )
    frames = frames.reshape(block_count * FRAMES, WINDOW)
    spectrum = jnp.dot(frames, dft_basis, precision=lax.Precision.HIGHEST)
    power_bins = spectrum[:, :BINS] * spectrum[:, :BINS] + spectrum[:, BINS:] * spectrum[:, BINS:]
    energy = jnp.dot(power_bins, filters, precision=lax.Precision.HIGHEST)
    features = (
        ((jnp.log10(energy + 1e-10) + 4.0) / 4.0)
        .astype(jnp.bfloat16)
        .reshape(block_count, FRAMES, MEL)
    )
    zero_mel = jnp.zeros((block_count, 1, MEL), jnp.bfloat16)
    padded = jnp.concatenate([zero_mel, features, zero_mel], axis=1)
    stacked = jnp.concatenate([padded[:, :-2], padded[:, 1:-1], padded[:, 2:]], axis=2).reshape(
        block_count * FRAMES, 3 * MEL
    )
    hidden = jax.nn.gelu(
        jnp.dot(stacked, conv_first, preferred_element_type=jnp.float32) + bias_first,
        approximate=False,
    )
    hidden = hidden.astype(jnp.bfloat16).reshape(block_count, FRAMES // 2, 2, WIDTH)
    even_rows = hidden[:, :, 0]
    odd_rows = hidden[:, :, 1]
    before = jnp.concatenate(
        [jnp.zeros((block_count, 1, WIDTH), jnp.bfloat16), odd_rows[:, :-1]], axis=1
    )
    second_in = jnp.concatenate([before, even_rows, odd_rows], axis=2).reshape(
        block_count * FRAMES // 2, 3 * WIDTH
    )
    activated = jax.nn.gelu(
        jnp.dot(second_in, conv_second, preferred_element_type=jnp.float32) + bias_second,
        approximate=False,
    )
    pooled = jnp.mean(activated.reshape(block_count, TOK, 2, WIDTH), axis=2)
    row_mean = jnp.mean(pooled, axis=-1, keepdims=True)
    centred = pooled - row_mean
    row_var = jnp.mean(centred * centred, axis=-1, keepdims=True)
    normed = centred / jnp.sqrt(row_var + 1e-05) * norm_gain
    return normed.astype(jnp.bfloat16).reshape(block_count * TOK, WIDTH)


def shards(
    waveforms,
    clip_lengths,
    block_starts,
    conv_first,
    bias_first,
    conv_second,
    bias_second,
    norm_gain,
    projector,
    proj_bias,
):
    tables = spectral_tables()
    devices_seq = lax.axis_size("seq")
    slots_all = waveforms.shape[1]
    lengths = clip_lengths[0]
    starts = block_starts[0]
    whole_first = lax.all_gather(conv_first, "batch", axis=0, tiled=True)
    blocks = waveforms[0]
    group_slot = jnp.arange(devices_seq * slots_all, dtype=jnp.int32)
    group_live = group_slot % slots_all < jnp.repeat(lengths, slots_all)
    token_rows = encode(
        blocks, tables, whole_first, bias_first, conv_second, bias_second, norm_gain
    )
    projected = (
        jnp.dot(
            lax.all_gather(token_rows, "seq", axis=0, tiled=True),
            projector,
            preferred_element_type=jnp.float32,
        )
        + proj_bias
    ).astype(jnp.bfloat16)
    total_rows = projected.shape[0]
    length_all = devices_seq * OWN_ROWS
    offsets = jnp.arange(TOK, dtype=jnp.int32)
    target = jnp.where(group_live[:, None], starts[:, None] + offsets[None, :], length_all).reshape(
        -1
    )
    row_index = (
        jnp.full((length_all,), total_rows, jnp.int32)
        .at[target]
        .set(jnp.arange(total_rows, dtype=jnp.int32), mode="drop")
    )
    padded_rows = jnp.concatenate(
        [projected, jnp.zeros((1, projected.shape[1]), jnp.bfloat16)], axis=0
    )
    placed = jnp.take(padded_rows, row_index, axis=0)
    owned_rows = lax.all_to_all(placed, "seq", split_axis=0, concat_axis=1, tiled=True)
    return owned_rows[None]


def solution(mesh):
    return jax.shard_map(
        shards,
        mesh=mesh,
        in_specs=(
            P("batch", "seq", None),
            P("batch", None),
            P("batch", None),
            P("batch", None),
            P(),
            P(),
            P(),
            P(),
            P(None, "seq"),
            P("seq"),
        ),
        out_specs=P("batch", "seq", None),
        check_vma=False,
    )
```

profile of v0, /device:TPU:0, one launch (start us, length us, event | category | flops | bytes accessed | tf_op | source)
XLA Modules:
  0.0 152.7 jit_solution(5425280199517510005)
XLA Ops:
  6.5 1.5 reshape.141
  8.2 0.5 pad_maximum_fusion
  8.6 0.6 copy-done.1
  9.3 2.4 %fusion.50 = f32[576,402]{0,1:T(8,128)S(1)} fusion(f32[576,400]{1,0:T(8,128)S(1)} %bitcast.32, f32[400,402]{1,0:T(8,128)S(1)} %copy-done.1), kind=kOutput, calls=%fused_computation.88 | convolution fusion | flops 1111449600 | bytes 2491008 | tf_op jit(solution)/shard_map/dot_general | solution.py:64
  11.7 1.2 fusion.30
  13.0 34.7 %all_gather.6 = bf16[384,1280]{1,0:T(8,128)(2,1)S(1)} all-gather(bf16[48,1280]{1,0:T(8,128)(2,1)S(1)} %copy-done.2), channel_id=1, replica_groups=mesh['seq'=4,'batch'=8] {'batch'}, dimensions={0}, use_global_device_ids=true | all-gather | bytes 1105920 | tf_op jit(solution)/shard_map/all_gather | solution.py:119
  47.7 7.8 %fusion.2 = bf16[576,1280]{1,0:T(8,128)(2,1)} fusion(bf16[384,1280]{1,0:T(8,128)(2,1)S(1)} %all_gather.6, f32[1280]{0:T(1024)S(1)} %copy-done.6, bf16[576,128]{1,0:T(8,128)(2,1)S(1)} %bitcast.39, bf16[576,128]{1,0:T(8,128)(2,1)S(1)} %fusion.30, bf16[576,128]{1,0:T(8,128)(2,1)S(1)} %bitcast.38), kind=kOutput, calls=%fused_computation.6 | convolution fusion | flops 616218624 | bytes 2905088 | tf_op jit(solution)/shard_map/dot_general | solution.py:78
  55.5 4.3 %reshape.139 = bf16[6,48,2,1280]{3,2,1,0:T(2,128)(2,1)} reshape(bf16[576,1280]{1,0:T(8,128)(2,1)} %fusion.2) | data formatting | bytes 2949120 | tf_op jit(solution)/shard_map/reshape | solution.py:81
  59.8 4.3 %fusion.48 = (bf16[6,48,1,1280]{3,2,1,0:T(2,128)(2,1)S(1)}, bf16[6,48,1,1280]{3,2,1,0:T(2,128)(2,1)S(1)}) fusion(bf16[6,48,2,1280]{3,2,1,0:T(2,128)(2,1)} %reshape.139), kind=kLoop, calls=%fused_computation.86 | loop fusion | bytes 2949120 | tf_op jit(solution)/shard_map/slice | solution.py:82
  64.6 0.4 copy-done.7
  65.0 10.8 %fusion.16 = f32[288,1280]{1,0:T(8,128)} fusion(bf16[3840,1280]{1,0:T(8,128)(2,1)} %param.17, bf16[288,1280]{1,0:T(8,128)(2,1)S(1)} %bitcast.34, bf16[288,1280]{1,0:T(8,128)(2,1)S(1)} %bitcast.35, bf16[288,1280]{1,0:T(8,128)(2,1)S(1)} %bitcast.36, f32[1280]{0:T(1024)S(1)} %copy-done.7), kind=kOutput, calls=%fused_computation.32 | convolution fusion | flops 2861752320 | bytes 13521920 | tf_op jit(solution)/shard_map/dot_general | solution.py:91
  75.9 3.0 %reshape.140 = f32[6,24,2,1280]{3,2,1,0:T(2,128)} reshape(f32[288,1280]{1,0:T(8,128)} %fusion.16) | data formatting | bytes 2949120 | tf_op jit(solution)/shard_map/reshape | solution.py:94
  78.9 3.1 %reduce_sum.27 = f32[6,24,1280]{2,1,0:T(8,128)S(1)} reduce(f32[6,24,2,1280]{3,2,1,0:T(2,128)} %reshape.140, f32[]{:T(128)} %constant.65.clone.1), dimensions={2}, to_apply=%region_1.2 | reduce | flops 184320 | bytes 2211844 | tf_op jit(solution)/shard_map/reduce_sum | solution.py:94
  82.2 0.9 multiply_reduce_fusion
  83.3 2.0 %fusion.33 = bf16[144,1280]{1,0:T(8,128)(2,1)} fusion(f32[6,24,1280]{2,1,0:T(8,128)} %get-tuple-element.8, f32[1280]{0:T(1024)S(1)} %copy-done.3, f32[144]{0:T(256)S(1)} %sqrt.12, f32[144]{0:T(256)S(1)} %div.33), kind=kLoop, calls=%fused_computation.58 | loop fusion | flops 737280 | bytes 1112192 | tf_op jit(solution)/shard_map/convert_element_type | solution.py:99
  85.7 4.1 %scatter_custom_fusion = s32[768]{0:T(1024)S(1)} fusion(s32[576]{0:T(1024)S(1)} %fusion.41, s32[576]{0:T(1024)S(1)} %iota.13, s32[]{:T(128)} %constant.45.clone.1), kind=kCustom, calls=%fused_computation.79 | custom fusion | bytes 3076 | tf_op jit(solution)/shard_map/scatter | solution.py:143
  89.9 15.4 %all-gather.2.cloned.1.call-done = bf16[576,1280]{1,0:T(8,128)(2,1)} async-done(((bf16[144,1280]{1,0:T(8,128)(2,1)}), bf16[576,1280]{1,0:T(8,128)(2,1)}) %all-gather.2.cloned.1.call-update) | async-done | bytes 1474576 | tf_op jit(solution)/shard_map/all_gather | solution.py:128
  105.3 3.1 %add_convert_fusion = bf16[576,1024]{1,0:T(8,128)(2,1)S(1)} fusion(bf16[576,1280]{1,0:T(8,128)(2,1)} %all-gather.2.cloned.1.call-done, bf16[1280,1024]{1,0:T(8,128)(2,1)S(1)} %copy-done, f32[1024]{0:T(1024)S(1)} %copy-done.8), kind=kOutput, calls=%fused_computation.23 | convolution fusion | flops 1511129088 | bytes 5279744 | tf_op jit(solution)/shard_map/dot_general | solution.py:127
  108.4 1.1 concatenate.45
  109.5 6.0 %gather_fusion = bf16[768,1024]{1,0:T(8,128)(2,1)} fusion(bf16[577,1024]{1,0:T(8,128)(2,1)} %concatenate.45, s32[1024]{0:T(1024)S(1)} %pad_clamp_fusion), kind=kCustom, calls=%fused_computation | custom fusion | bytes 3148800 | tf_op jit(solution)/shard_map/jit(_take)/gather | solution.py:148
  115.5 1.6 %broadcast_select_fusion = bf16[4,192,1024]{2,1,0:T(8,128)(2,1)S(1)} fusion(bf16[4,192,1024]{2,1,0:T(8,128)(2,1)} %bitcast.31, pred[4,192]{1,0:T(4,128)(4,1)S(1)} %broadcast_in_dim.54), kind=kLoop, calls=%fused_computation.30 | loop fusion | flops 786432 | bytes 3146496 | tf_op jit(solution)/shard_map/jit(_take)/select_n | solution.py:148
  117.1 22.5 %all_to_all.13 = bf16[4,192,1024]{2,1,0:T(8,128)(2,1)S(1)} all-to-all(bf16[4,192,1024]{2,1,0:T(8,128)(2,1)S(1)} %broadcast_select_fusion), channel_id=1, replica_groups=mesh['seq'=4,'batch'=8] {'seq'}, dimensions={0} | all-to-all | bytes 3145728 | tf_op jit(solution)/shard_map/all_to_all | solution.py:149
  139.6 2.4 %copy.19 = bf16[192,4,1024]{2,1,0:T(4,128)(2,1)} copy(bf16[192,4,1024]{2,0,1:T(8,128)(2,1)S(1)} %bitcast.30) | data formatting | bytes 3145728 | tf_op jit(solution)/shard_map/all_to_all | solution.py:149
  142.0 3.8 %broadcast_in_dim.58 = bf16[1,192,4096]{2,1,0:T(8,128)(2,1)} reshape(bf16[192,4,1024]{2,1,0:T(4,128)(2,1)} %copy.19) | data formatting | bytes 3145728 | tf_op jit(solution)/shard_map/broadcast_in_dim | solution.py:150
  (43 shorter events, 1.4 us)
Async XLA Ops:
  6.5 98.8 %copy-start = (bf16[1280,1024]{1,0:T(8,128)(2,1)S(1)}, bf16[1280,1024]{1,0:T(8,128)(2,1)}, u32[]{:S(2)}) copy-start(bf16[1280,1024]{1,0:T(8,128)(2,1)} %param.20) | copy-start | bytes 7864324
  6.5 98.8 %all-gather.2.cloned.1.call-start = ((), (), s32[]{:S(2)}) async-start(), calls=%async_computation.1 | async-start | bytes 1843200 | tf_op jit(solution)/shard_map/all_gather | solution.py:128
  8.1 1.1 copy-start.1
  8.6 3.0 %copy-start.9 = (f32[201,128]{1,0:T(8,128)S(1)}, f32[201,128]{1,0:T(8,128)}, u32[]{:S(2)}) copy-start(f32[201,128]{1,0:T(8,128)} %constant.21.clone) | copy-start | bytes 308740
  11.7 1.3 copy-start.2
  11.7 36.0 %copy-start.6 = (f32[1280]{0:T(1024)S(1)}, f32[1280]{0:T(1024)}, u32[]{:S(2)}) copy-start(f32[1280]{0:T(1024)} %param.16) | copy-start | bytes 15364
  64.3 0.7 copy-start.7
  82.0 1.3 copy-start.3
  82.1 3.2 %copy-start.4 = (s32[1,4]{1,0:T(1,128)S(1)}, s32[1,4]{1,0:T(1,128)}, u32[]{:S(2)}) copy-start(s32[1,4]{1,0:T(1,128)} %param.13) | copy-start | bytes 52
  82.2 3.4 %copy-start.5 = (s32[1,24]{1,0:T(1,128)S(1)}, s32[1,24]{1,0:T(1,128)}, u32[]{:S(2)}) copy-start(s32[1,24]{1,0:T(1,128)} %param.14) | copy-start | bytes 292
  82.2 23.2 %copy-start.8 = (f32[1024]{0:T(1024)S(1)}, f32[1024]{0:T(1024)}, u32[]{:S(2)}) copy-start(f32[1024]{0:T(1024)} %param.21) | copy-start | bytes 12292
Sparse Core Ops, SparseCore 0:
  85.5 19.8 all-gather.1
where the time goes:
time: 153 us
  blocking collectives  57.2 us (37%)
  local copies, waits for them, and re-layouts  32.6 us (21%)
  matrix products  25.3 us (17%)
  waiting for transfers between devices  15.4 us (10%)
  between operations  13.7 us (9%)
  other arithmetic  8.41 us (5%)
    all_gather x1, blocking collectives, shards(): whole_first = lax.all_gather(conv_first, 'batch', axis=0, tiled=True)  34.7 us
    all_to_all x1, blocking collectives, shards(): lax.all_to_all(placed, 'seq', split_axis=0, concat_axis=1, tiled=True)  22.5 us
    all_gather x1, waiting for transfers between devices, shards(): lax.all_gather(token_rows, 'seq', axis=0, tiled=True)  15.4 us
    dot_general x1, matrix products, encode(): jnp.dot(second_in, conv_second, preferred_element_type=jnp.float32)  10.8 us
    dot_general x1, matrix products, encode(): jnp.dot(stacked, conv_first, preferred_element_type=jnp.float32)  7.85 us
    gather x1, local copies, waits for them, and re-layouts, shards(): placed = jnp.take(padded_rows, row_index, axis=0)  5.97 us
    reshape x1, local copies, waits for them, and re-layouts, encode(): hidden.astype(jnp.bfloat16).reshape(block_count, FRAMES // 2, 2, WIDTH)  4.31 us
    slice x1, local copies, waits for them, and re-layouts, encode(): even_rows = hidden[:, :, 0]  4.28 us
  transfers between devices with their start and end apart: 1, of which 1 were waited for; matrix products, arithmetic and copies ran while one was open for 3% of the time, Pallas kernels for 0%

commit v1 on v0

--- a/solution.py
+++ b/solution.py
@@ -116,7 +116,17 @@
     slots_all = waveforms.shape[1]
     lengths = clip_lengths[0]
     starts = block_starts[0]
-    whole_first = lax.all_gather(conv_first, "batch", axis=0, tiled=True)
+    peers, position, span = (lax.axis_size("batch"), lax.axis_index("batch"), conv_first.shape[0])
+    upward = [(i, (i + 1) % peers) for i in range(peers)]
+    whole_first = jnp.zeros(
+        (*conv_first.shape[:0], peers * span, *conv_first.shape[0 + 1 :]), conv_first.dtype
+    )
+    current = conv_first
+    for step in range(peers):
+        source = (position - step) % peers
+        whole_first = lax.dynamic_update_slice_in_dim(whole_first, current, source * span, axis=0)
+        if step < peers - 1:
+            current = lax.ppermute(current, "batch", upward)
     blocks = waveforms[0]
     group_slot = jnp.arange(devices_seq * slots_all, dtype=jnp.int32)
     group_live = group_slot % slots_all < jnp.repeat(lengths, slots_all)

time: 153 us -> 169 us (1.10)
  waiting for transfers between devices: 15.4 us -> 52.1 us
  blocking collectives: 57.2 us -> 22.5 us
  local copies, waits for them, and re-layouts: 32.6 us -> 40.5 us
  starting transfers between devices: 0.01 us -> 4.58 us
    ppermute x0 -> x7, waiting for transfers between devices: none -> 40.1 us  [shards(): current = lax.ppermute(current, 'batch', upward)]
    all_gather x1 -> x0, blocking collectives: 34.7 us -> none  [shards(): whole_first = lax.all_gather(conv_first, 'batch', axis=0, tiled=True)]
    dynamic_update_slice x0 -> x8, local copies, waits for them, and re-layouts: none -> 6.56 us  [shards(): lax.dynamic_update_slice_in_dim(whole_first, current, source * span, axis=0)]
    ppermute x0 -> x7, starting transfers between devices: none -> 4.58 us  [shards(): current = lax.ppermute(current, 'batch', upward)]
    all_gather x1, waiting for transfers between devices: 15.4 us -> 11.9 us  [shards(): lax.all_gather(token_rows, 'seq', axis=0, tiled=True)]
  transfers between devices with their start and end apart: 1 -> 8, of which waited for: 1 -> 7; matrix products, arithmetic and copies ran while one was open for 3% -> 10% of each run, Pallas kernels for 0% -> 0%
where the time goes in v1:
time: 169 us; the launch traced here: 168 us
  waiting for transfers between devices  52.1 us (31%)
  local copies, waits for them, and re-layouts  40.5 us (24%)
  matrix products  26.5 us (16%)
  blocking collectives  22.5 us (13%)
  between operations  13.8 us (8%)
  other arithmetic  8.41 us (5%)
  starting transfers between devices  4.58 us (3%)
    ppermute x7, waiting for transfers between devices, shards(): current = lax.ppermute(current, 'batch', upward)  40.1 us
    all_to_all x1, blocking collectives, shards(): lax.all_to_all(placed, 'seq', split_axis=0, concat_axis=1, tiled=True)  22.5 us
    all_gather x1, waiting for transfers between devices, shards(): lax.all_gather(token_rows, 'seq', axis=0, tiled=True)  11.9 us
    dot_general x1, matrix products, encode(): jnp.dot(second_in, conv_second, preferred_element_type=jnp.float32)  10.8 us
    dot_general x1, matrix products, encode(): jnp.dot(stacked, conv_first, preferred_element_type=jnp.float32)  9.05 us
    dynamic_update_slice x8, local copies, waits for them, and re-layouts, shards(): lax.dynamic_update_slice_in_dim(whole_first, current, source * span, axis=0)  6.56 us
    gather x1, local copies, waits for them, and re-layouts, shards(): placed = jnp.take(padded_rows, row_index, axis=0)  5.97 us
    ppermute x7, starting transfers between devices, shards(): current = lax.ppermute(current, 'batch', upward)  4.58 us
  transfers between devices with their start and end apart: 8, of which 7 were waited for; matrix products, arithmetic and copies ran while one was open for 10% of the time, Pallas kernels for 0%

profile of v1, /device:TPU:0, one launch (start us, length us, event | category | flops | bytes accessed | tf_op | source)
XLA Modules:
  0.0 168.5 jit_solution(12439483199741570245)
XLA Ops:
  6.5 3.0 %collective-permute-start = (bf16[48,1280]{1,0:T(8,128)(2,1)}, bf16[48,1280]{1,0:T(8,128)(2,1)}, u32[]{:S(2)}, u32[]{:S(2)}) collective-permute-start(bf16[48,1280]{1,0:T(8,128)(2,1)} %param.15), channel_id=1, source_target_pairs={{0,1},{1,2},{2,3},{3,4},{4,5},{5,6},{6,7},{7,0},{8,9},{9,10},{10,1... | collective-permute-start | bytes 368648 | tf_op jit(solution)/shard_map/ppermute | solution.py:129
  14.6 2.4 %fusion.50 = f32[576,402]{0,1:T(8,128)S(1)} fusion(f32[576,400]{1,0:T(8,128)S(1)} %bitcast.32, f32[400,402]{1,0:T(8,128)S(1)} %copy-done.4), kind=kOutput, calls=%fused_computation.96 | convolution fusion | flops 1111449600 | bytes 2491008 | tf_op jit(solution)/shard_map/dot_general | solution.py:64
  18.4 1.6 collective-permute-start.1
  21.6 4.6 %collective-permute-done.1 = bf16[48,1280]{1,0:T(8,128)(2,1)S(1)} collective-permute-done((bf16[48,1280]{1,0:T(8,128)(2,1)}, bf16[48,1280]{1,0:T(8,128)(2,1)S(1)}, u32[]{:S(2)}, u32[]{:S(2)}) %collective-permute-start.1) | collective-permute-done | bytes 122912 | tf_op jit(solution)/shard_map/ppermute | solution.py:129
  26.9 6.9 %collective-permute-done.2 = bf16[48,1280]{1,0:T(8,128)(2,1)S(1)} collective-permute-done((bf16[48,1280]{1,0:T(8,128)(2,1)S(1)}, bf16[48,1280]{1,0:T(8,128)(2,1)S(1)}, u32[]{:S(2)}, u32[]{:S(2)}) %collective-permute-start.2) | collective-permute-done | bytes 122912 | tf_op jit(solution)/shard_map/ppermute | solution.py:129
  34.5 6.9 %collective-permute-done.3 = bf16[48,1280]{1,0:T(8,128)(2,1)S(1)} collective-permute-done((bf16[48,1280]{1,0:T(8,128)(2,1)S(1)}, bf16[48,1280]{1,0:T(8,128)(2,1)S(1)}, u32[]{:S(2)}, u32[]{:S(2)}) %collective-permute-start.3) | collective-permute-done | bytes 122912 | tf_op jit(solution)/shard_map/ppermute | solution.py:129
  42.1 6.9 %collective-permute-done.4 = bf16[48,1280]{1,0:T(8,128)(2,1)S(1)} collective-permute-done((bf16[48,1280]{1,0:T(8,128)(2,1)S(1)}, bf16[48,1280]{1,0:T(8,128)(2,1)S(1)}, u32[]{:S(2)}, u32[]{:S(2)}) %collective-permute-start.4) | collective-permute-done | bytes 122912 | tf_op jit(solution)/shard_map/ppermute | solution.py:129
  49.6 7.8 %collective-permute-done.5 = bf16[48,1280]{1,0:T(8,128)(2,1)S(1)} collective-permute-done((bf16[48,1280]{1,0:T(8,128)(2,1)S(1)}, bf16[48,1280]{1,0:T(8,128)(2,1)S(1)}, u32[]{:S(2)}, u32[]{:S(2)}) %collective-permute-start.5) | collective-permute-done | bytes 122912 | tf_op jit(solution)/shard_map/ppermute | solution.py:129
  58.1 6.9 %collective-permute-done.6 = bf16[48,1280]{1,0:T(8,128)(2,1)S(1)} collective-permute-done((bf16[48,1280]{1,0:T(8,128)(2,1)S(1)}, bf16[48,1280]{1,0:T(8,128)(2,1)S(1)}, u32[]{:S(2)}, u32[]{:S(2)}) %collective-permute-start.6) | collective-permute-done | bytes 122912 | tf_op jit(solution)/shard_map/ppermute | solution.py:129
  65.7 9.1 %fusion.2 = bf16[576,1280]{1,0:T(8,128)(2,1)} fusion(bf16[384,1280]{1,0:T(8,128)(2,1)} %constant_dynamic-update-slice_fusion, f32[1280]{0:T(1024)S(1)} %copy-done.8, bf16[576,128]{1,0:T(8,128)(2,1)S(1)} %bitcast.39, bf16[576,128]{1,0:T(8,128)(2,1)S(1)} %fusion.30, bf16[576,128]{1,0:T(8,128)(2,1)S(1)} %bitcast.38), kind=kOutput, calls=%fused_computation.6 | convolution fusion | flops 616218624 | bytes 2905088 | tf_op jit(solution)/shard_map/dot_general | solution.py:78
  74.8 4.3 %reshape.139 = bf16[6,48,2,1280]{3,2,1,0:T(2,128)(2,1)} reshape(bf16[576,1280]{1,0:T(8,128)(2,1)} %fusion.2) | data formatting | bytes 2949120 | tf_op jit(solution)/shard_map/reshape | solution.py:81
  79.1 4.3 %fusion.48 = (bf16[6,48,1,1280]{3,2,1,0:T(2,128)(2,1)S(1)}, bf16[6,48,1,1280]{3,2,1,0:T(2,128)(2,1)S(1)}) fusion(bf16[6,48,2,1280]{3,2,1,0:T(2,128)(2,1)} %reshape.139), kind=kLoop, calls=%fused_computation.94 | loop fusion | bytes 2949120 | tf_op jit(solution)/shard_map/slice | solution.py:82
  84.3 10.8 %fusion.16 = f32[288,1280]{1,0:T(8,128)} fusion(bf16[3840,1280]{1,0:T(8,128)(2,1)} %param.17, bf16[288,1280]{1,0:T(8,128)(2,1)S(1)} %bitcast.34, bf16[288,1280]{1,0:T(8,128)(2,1)S(1)} %bitcast.36, bf16[288,1280]{1,0:T(8,128)(2,1)S(1)} %bitcast.35, f32[1280]{0:T(1024)S(1)} %copy-done.9), kind=kOutput, calls=%fused_computation.32 | convolution fusion | flops 2861752320 | bytes 13521920 | tf_op jit(solution)/shard_map/dot_general | solution.py:91
  95.1 3.0 %reshape.140 = f32[6,24,2,1280]{3,2,1,0:T(2,128)} reshape(f32[288,1280]{1,0:T(8,128)} %fusion.16) | data formatting | bytes 2949120 | tf_op jit(solution)/shard_map/reshape | solution.py:94
  98.1 3.1 %reduce_sum.27 = f32[6,24,1280]{2,1,0:T(8,128)S(1)} reduce(f32[6,24,2,1280]{3,2,1,0:T(2,128)} %reshape.140, f32[]{:T(128)} %constant.95.clone.1), dimensions={2}, to_apply=%region_1.2 | reduce | flops 184320 | bytes 2211844 | tf_op jit(solution)/shard_map/reduce_sum | solution.py:94
  102.5 2.0 %fusion.33 = bf16[144,1280]{1,0:T(8,128)(2,1)} fusion(f32[6,24,1280]{2,1,0:T(8,128)} %get-tuple-element.8, f32[1280]{0:T(1024)S(1)} %copy-done.5, f32[144]{0:T(256)S(1)} %sqrt.12, f32[144]{0:T(256)S(1)} %div.33), kind=kLoop, calls=%fused_computation.58 | loop fusion | flops 737280 | bytes 1112192 | tf_op jit(solution)/shard_map/convert_element_type | solution.py:99
  105.0 4.1 %scatter_custom_fusion = s32[768]{0:T(1024)S(1)} fusion(s32[576]{0:T(1024)S(1)} %fusion.41, s32[576]{0:T(1024)S(1)} %iota.13, s32[]{:T(128)} %constant.61.clone.1), kind=kCustom, calls=%fused_computation.87 | custom fusion | bytes 3076 | tf_op jit(solution)/shard_map/scatter | solution.py:153
  109.2 11.9 %all-gather.2.cloned.1.call-done = bf16[576,1280]{1,0:T(8,128)(2,1)} async-done(((bf16[144,1280]{1,0:T(8,128)(2,1)}), bf16[576,1280]{1,0:T(8,128)(2,1)}) %all-gather.2.cloned.1.call-update) | async-done | bytes 1474576 | tf_op jit(solution)/shard_map/all_gather | solution.py:138
  121.1 3.1 %add_convert_fusion = bf16[576,1024]{1,0:T(8,128)(2,1)S(1)} fusion(bf16[576,1280]{1,0:T(8,128)(2,1)} %all-gather.2.cloned.1.call-done, bf16[1280,1024]{1,0:T(8,128)(2,1)S(1)} %copy-done, f32[1024]{0:T(1024)S(1)} %copy-done.10), kind=kOutput, calls=%fused_computation.23 | convolution fusion | flops 1511129088 | bytes 5279744 | tf_op jit(solution)/shard_map/dot_general | solution.py:137
  125.3 6.0 %gather_fusion = bf16[768,1024]{1,0:T(8,128)(2,1)} fusion(bf16[577,1024]{1,0:T(8,128)(2,1)} %concatenate.45, s32[1024]{0:T(1024)S(1)} %pad_clamp_fusion), kind=kCustom, calls=%fused_computation | custom fusion | bytes 3148800 | tf_op jit(solution)/shard_map/jit(_take)/gather | solution.py:158
  131.3 1.6 broadcast_select_fusion
  132.9 22.5 %all_to_all.13 = bf16[4,192,1024]{2,1,0:T(8,128)(2,1)S(1)} all-to-all(bf16[4,192,1024]{2,1,0:T(8,128)(2,1)S(1)} %broadcast_select_fusion), channel_id=1, replica_groups=mesh['seq'=4,'batch'=8] {'seq'}, dimensions={0} | all-to-all | bytes 3145728 | tf_op jit(solution)/shard_map/all_to_all | solution.py:159
  155.4 2.4 %copy.19 = bf16[192,4,1024]{2,1,0:T(4,128)(2,1)} copy(bf16[192,4,1024]{2,0,1:T(8,128)(2,1)S(1)} %bitcast.30) | data formatting | bytes 3145728 | tf_op jit(solution)/shard_map/all_to_all | solution.py:159
  157.8 3.8 %broadcast_in_dim.62 = bf16[1,192,4096]{2,1,0:T(8,128)(2,1)} reshape(bf16[192,4,1024]{2,1,0:T(4,128)(2,1)} %copy.19) | data formatting | bytes 3145728 | tf_op jit(solution)/shard_map/broadcast_in_dim | solution.py:160
  (69 shorter events, 15.5 us)
Async XLA Ops:
  6.5 114.6 %copy-start = (bf16[1280,1024]{1,0:T(8,128)(2,1)S(1)}, bf16[1280,1024]{1,0:T(8,128)(2,1)}, u32[]{:S(2)}) copy-start(bf16[1280,1024]{1,0:T(8,128)(2,1)} %param.20) | copy-start | bytes 7864324
  6.5 114.6 %all-gather.2.cloned.1.call-start = ((), (), s32[]{:S(2)}) async-start(), calls=%async_computation.1 | async-start | bytes 1843200 | tf_op jit(solution)/shard_map/all_gather | solution.py:138
  6.5 11.9 %collective-permute-start = (bf16[48,1280]{1,0:T(8,128)(2,1)}, bf16[48,1280]{1,0:T(8,128)(2,1)}, u32[]{:S(2)}, u32[]{:S(2)}) collective-permute-start(bf16[48,1280]{1,0:T(8,128)(2,1)} %param.15), channel_id=1, source_target_pairs={{0,1},{1,2},{2,3},{3,4},{4,5},{5,6},{6,7},{7,0},{8,9},{9,10},{10,1... | collective-permute-start | bytes 368648 | tf_op jit(solution)/shard_map/ppermute | solution.py:129
  12.0 2.1 %copy-start.1 = (f32[6,96,160]{2,1,0:T(8,128)S(1)}, f32[6,96,160]{2,1,0:T(8,128)}, u32[]{:S(2)}) copy-start(f32[6,96,160]{2,1,0:T(8,128)} %get-tuple-element.9) | copy-start | bytes 1105924
  12.0 2.1 %copy-start.2 = (f32[6,96,160]{2,1,0:T(8,128)S(1)}, f32[6,96,160]{2,1,0:T(8,128)}, u32[]{:S(2)}) copy-start(f32[6,96,160]{2,1,0:T(8,128)} %get-tuple-element.10) | copy-start | bytes 1105924
  12.1 2.5 %copy-start.4 = (f32[400,402]{1,0:T(8,128)S(1)}, f32[400,402]{1,0:T(8,128)}, u32[]{:S(2)}) copy-start(f32[400,402]{1,0:T(8,128)} %constant.217.clone) | copy-start | bytes 1929604
  13.1 1.0 copy-start.3
  14.6 2.4 %copy-start.11 = (f32[201,128]{1,0:T(8,128)S(1)}, f32[201,128]{1,0:T(8,128)}, u32[]{:S(2)}) copy-start(f32[201,128]{1,0:T(8,128)} %constant.218.clone) | copy-start | bytes 308740
  17.0 48.7 %copy-start.8 = (f32[1280]{0:T(1024)S(1)}, f32[1280]{0:T(1024)}, u32[]{:S(2)}) copy-start(f32[1280]{0:T(1024)} %param.16) | copy-start | bytes 15364
  18.4 7.8 %collective-permute-start.1 = (bf16[48,1280]{1,0:T(8,128)(2,1)}, bf16[48,1280]{1,0:T(8,128)(2,1)S(1)}, u32[]{:S(2)}, u32[]{:S(2)}) collective-permute-start(bf16[48,1280]{1,0:T(8,128)(2,1)} %collective-permute-done), channel_id=1, source_target_pairs={{0,1},{1,2},{2,3},{3,4},{4,5},{5,6},{6,7},{7,0},{8,9},{9,10},{10,1... | collective-permute-start | bytes 368648 | tf_op jit(solution)/shard_map/ppermute | solution.py:129
  26.3 7.6 %collective-permute-start.2 = (bf16[48,1280]{1,0:T(8,128)(2,1)S(1)}, bf16[48,1280]{1,0:T(8,128)(2,1)S(1)}, u32[]{:S(2)}, u32[]{:S(2)}) collective-permute-start(bf16[48,1280]{1,0:T(8,128)(2,1)S(1)} %collective-permute-done.1), channel_id=1, source_target_pairs={{0,1},{1,2},{2,3},{3,4},{4,5},{5,6},{6,7},{7,0},{8,9},{9,10},{10,1... | collective-permute-start | bytes 368648 | tf_op jit(solution)/shard_map/ppermute | solution.py:129
  33.8 7.6 %collective-permute-start.3 = (bf16[48,1280]{1,0:T(8,128)(2,1)S(1)}, bf16[48,1280]{1,0:T(8,128)(2,1)S(1)}, u32[]{:S(2)}, u32[]{:S(2)}) collective-permute-start(bf16[48,1280]{1,0:T(8,128)(2,1)S(1)} %collective-permute-done.2), channel_id=1, source_target_pairs={{0,1},{1,2},{2,3},{3,4},{4,5},{5,6},{6,7},{7,0},{8,9},{9,10},{10,1... | collective-permute-start | bytes 368648 | tf_op jit(solution)/shard_map/ppermute | solution.py:129
  41.4 7.6 %collective-permute-start.4 = (bf16[48,1280]{1,0:T(8,128)(2,1)S(1)}, bf16[48,1280]{1,0:T(8,128)(2,1)S(1)}, u32[]{:S(2)}, u32[]{:S(2)}) collective-permute-start(bf16[48,1280]{1,0:T(8,128)(2,1)S(1)} %collective-permute-done.3), channel_id=1, source_target_pairs={{0,1},{1,2},{2,3},{3,4},{4,5},{5,6},{6,7},{7,0},{8,9},{9,10},{10,1... | collective-permute-start | bytes 368648 | tf_op jit(solution)/shard_map/ppermute | solution.py:129
  49.0 8.5 %collective-permute-start.5 = (bf16[48,1280]{1,0:T(8,128)(2,1)S(1)}, bf16[48,1280]{1,0:T(8,128)(2,1)S(1)}, u32[]{:S(2)}, u32[]{:S(2)}) collective-permute-start(bf16[48,1280]{1,0:T(8,128)(2,1)S(1)} %collective-permute-done.4), channel_id=1, source_target_pairs={{0,1},{1,2},{2,3},{3,4},{4,5},{5,6},{6,7},{7,0},{8,9},{9,10},{10,1... | collective-permute-start | bytes 368648 | tf_op jit(solution)/shard_map/ppermute | solution.py:129
  57.5 7.6 %collective-permute-start.6 = (bf16[48,1280]{1,0:T(8,128)(2,1)S(1)}, bf16[48,1280]{1,0:T(8,128)(2,1)S(1)}, u32[]{:S(2)}, u32[]{:S(2)}) collective-permute-start(bf16[48,1280]{1,0:T(8,128)(2,1)S(1)} %collective-permute-done.5), channel_id=1, source_target_pairs={{0,1},{1,2},{2,3},{3,4},{4,5},{5,6},{6,7},{7,0},{8,9},{9,10},{10,1... | collective-permute-start | bytes 368648 | tf_op jit(solution)/shard_map/ppermute | solution.py:129
  83.6 0.7 copy-start.9
  101.3 1.3 copy-start.5
  101.4 3.2 %copy-start.6 = (s32[1,4]{1,0:T(1,128)S(1)}, s32[1,4]{1,0:T(1,128)}, u32[]{:S(2)}) copy-start(s32[1,4]{1,0:T(1,128)} %param.13) | copy-start | bytes 52
  101.4 3.4 %copy-start.7 = (s32[1,24]{1,0:T(1,128)S(1)}, s32[1,24]{1,0:T(1,128)}, u32[]{:S(2)}) copy-start(s32[1,24]{1,0:T(1,128)} %param.14) | copy-start | bytes 292
  101.4 19.7 %copy-start.10 = (f32[1024]{0:T(1024)S(1)}, f32[1024]{0:T(1024)}, u32[]{:S(2)}) copy-start(f32[1024]{0:T(1024)} %param.21) | copy-start | bytes 12292
Sparse Core Ops, SparseCore 0:
  104.7 16.3 all-gather.1
